TPU v7x, 256 devices: a whole 4x4x8 slice. The times are simulated.
256 devices in a mesh: section: 16 (over y_hi, x, core), ray: 8 (over z), dp: 2 (over y_lo).
Axes of the slice: x: 4, y: 4 (y_hi: 2, y_lo: 2; y = y_hi * 2 + y_lo), z: 8, core: 2. Of those that a mesh axis runs over, the one named last changes fastest.
Arguments:
- section_tokens: bfloat16 [16, 2, 1024, 1024], P('section', 'dp', 'ray'), may hold values from -6 to 6
- enc_ln1: float32 [16, 1024], P('section'), may hold values from 0.5 to 1.5
- enc_qkv: bfloat16 [16, 1024, 3, 1024], P('section', None, None, 'ray'), may hold values from -40 to 40
- enc_out: bfloat16 [16, 1024, 1024], P('section', 'ray'), may hold values from -0.1875 to 0.1875
- enc_ln2: float32 [16, 1024], P('section'), may hold values from 0.5 to 1.5
- enc_up: bfloat16 [16, 1024, 4096], P('section', None, 'ray'), may hold values from -0.1875 to 0.1875
- enc_down: bfloat16 [16, 4096, 1024], P('section', 'ray'), may hold values from -0.09375 to 0.09375
- set_latent: bfloat16 [2, 1024, 1024], P('dp', 'ray'), may hold values from -6 to 6
- ray_queries: bfloat16 [2, 32768, 1024], P('dp', ('section', 'ray')), may hold values from -6 to 6
- dec_query: bfloat16 [1024, 1024], P('section'), may hold values from -40 to 40
- dec_kv: bfloat16 [1024, 2, 1024], P('section'), may hold values from -1 to 1
- dec_out: bfloat16 [1024, 1024], P('section'), may hold values from -0.1875 to 0.1875
- feature_grad: bfloat16 [2, 32768, 1024], P('dp', ('section', 'ray')), may hold values from -2 to 2
Outputs:
- handed: bfloat16 [16, 2, 1024, 1024], P('section', 'dp', 'ray')
- finished: bfloat16 [2, 1024, 1024], P('dp', 'ray', 'section')
- ray_features: bfloat16 [2, 32768, 1024], P('dp', ('section', 'ray'))
- latent_grad: bfloat16 [2, 1024, 1024], P('dp', 'ray')
- out_grad: float32 [1024, 1024], replicated
All inputs are finite; a program needn't handle non-finite values.
Results may differ from a plain program's by a relative error of at most 0.022.
The roundings to bfloat16 on the way count: a program that leaves them out, or rounds other values in their place, can miss the bound.
Values may be sent and summed in bfloat16 or wider, within the bound.
No kernel may reach another device: no remote copies, remote signals or barrier semaphores. Data moves between devices by JAX's collectives and lax.ppermute only.
A program may use at most 128 MiB of HBM per device.

v0:
```python
import math
import jax
import jax.numpy as jnp
from jax import lax
from jax.sharding import PartitionSpec as P

HEADS = 16


def shifted(value, axis, by):
    count = lax.axis_size(axis)
    pairs = [(i, i + by) for i in range(count) if 0 <= i + by < count]
    return lax.ppermute(value, axis, pairs)


def spread_2(value, axis, root):
    mine = lax.axis_index(axis) == root
    return lax.psum(jnp.where(mine, value, jnp.zeros_like(value)), axis)


def layer_norm(values, gain):
    values = values.astype(jnp.float32)
    center = values - jnp.mean(values, -1, keepdims=True)
    spread = jnp.mean(center * center, -1, keepdims=True)
    return center * lax.rsqrt(spread + 1e-05) * gain


def softmax_rows(scores):
    top = jnp.max(scores, -1, keepdims=True)
    expo = jnp.exp(scores - top)
    return expo / jnp.sum(expo, -1, keepdims=True)


def attend_heads(packed, head_dim):
    length = packed.shape[0]
    heads = packed.shape[1] // (3 * head_dim)
    split = packed.reshape(length, 3, heads, head_dim)
    scores = jnp.einsum(
        "qhd,khd->hqk", split[:, 0], split[:, 1], preferred_element_type=jnp.float32
    ) / math.sqrt(head_dim)
    probs = softmax_rows(scores).astype(jnp.bfloat16)
    mixed = jnp.einsum("hqk,khd->qhd", probs, split[:, 2], preferred_element_type=jnp.float32)
    return mixed.astype(jnp.bfloat16).reshape(length, heads * head_dim)


def latent_rows(pair_sum, w_pairs):
    result = lax.dot_general(
        pair_sum[:, 0],
        w_pairs[:, 0, :],
        (((1,), (1,)), ((), ())),
        preferred_element_type=jnp.float32,
    )
    result = result + lax.dot_general(
        pair_sum[:, 1],
        w_pairs[:, 1, :],
        (((1,), (1,)), ((), ())),
        preferred_element_type=jnp.float32,
    )
    return result.astype(jnp.bfloat16)


def local(
    section_tokens,
    enc_ln1,
    enc_qkv,
    enc_out,
    enc_ln2,
    enc_up,
    enc_down,
    set_latent,
    ray_queries,
    dec_query,
    dec_kv,
    dec_out,
    feature_grad,
):
    tokens = section_tokens[0, 0]
    width = tokens.shape[1]
    head_dim = width // HEADS
    local_width = enc_out.shape[1]
    w_qkv = enc_qkv[0].reshape(width, 3 * local_width)
    w_attn_out = enc_out[0]
    w_upper = enc_up[0]
    w_lower = enc_down[0]
    gain_one = enc_ln1[0]
    gain_two = enc_ln2[0]
    normed = layer_norm(tokens, gain_one).astype(jnp.bfloat16)
    packed = jnp.dot(
        lax.all_gather(normed, "ray", axis=0, tiled=True), w_qkv, preferred_element_type=jnp.float32
    ).astype(jnp.bfloat16)
    mixed = attend_heads(packed, head_dim)
    attn_rows = lax.psum_scatter(
        jnp.dot(mixed, w_attn_out, preferred_element_type=jnp.float32).astype(jnp.bfloat16),
        "ray",
        scatter_dimension=0,
        tiled=True,
    ).astype(jnp.float32)
    hidden = (tokens.astype(jnp.float32) + attn_rows).astype(jnp.bfloat16)
    upper = jax.nn.gelu(
        jnp.dot(
            lax.all_gather(
                layer_norm(hidden, gain_two).astype(jnp.bfloat16), "ray", axis=0, tiled=True
            ),
            w_upper,
            preferred_element_type=jnp.float32,
        ),
        approximate=True,
    ).astype(jnp.bfloat16)
    lower_rows = lax.psum_scatter(
        jnp.dot(upper, w_lower, preferred_element_type=jnp.float32).astype(jnp.bfloat16),
        "ray",
        scatter_dimension=0,
        tiled=True,
    ).astype(jnp.float32)
    layer_out = (hidden.astype(jnp.float32) + lower_rows).astype(jnp.bfloat16)
    handed = shifted(layer_out, "section", 1)
    finished_all = spread_2(layer_out, "section", lax.axis_size("section") - 1)
    columns = width // lax.axis_size("section")
    finished = lax.dynamic_slice_in_dim(
        finished_all, lax.axis_index("section") * columns, columns, 1
    )
    w_query, w_pairs, w_mix = (
        lax.all_gather(dec_query, "section", axis=0, tiled=True),
        lax.all_gather(dec_kv, "section", axis=0, tiled=True),
        lax.all_gather(dec_out, "section", axis=0, tiled=True),
    )
    latent = set_latent[0]
    queries = ray_queries[0]
    cotangent = feature_grad[0]
    flat_pairs = w_pairs.reshape(width, 2 * width)
    key_values = lax.all_gather(
        jnp.dot(latent, flat_pairs, preferred_element_type=jnp.float32).astype(jnp.bfloat16),
        "ray",
        axis=0,
        tiled=True,
    )
    scene_len = key_values.shape[0]
    ray_rows = queries.shape[0]
    scale = 1.0 / math.sqrt(head_dim)
    keys = key_values[:, :width].reshape(scene_len, HEADS, head_dim)
    values = key_values[:, width:].reshape(scene_len, HEADS, head_dim)
    query = (
        jnp.dot(queries, w_query, preferred_element_type=jnp.float32)
        .astype(jnp.bfloat16)
        .reshape(ray_rows, HEADS, head_dim)
    )
    scores = jnp.einsum("rhd,lhd->hrl", query, keys, preferred_element_type=jnp.float32) * scale
    probs = softmax_rows(scores)
    probs_low = probs.astype(jnp.bfloat16)
    attended = (
        jnp.einsum("hrl,lhd->rhd", probs_low, values, preferred_element_type=jnp.float32)
        .astype(jnp.bfloat16)
        .reshape(ray_rows, width)
    )
    features = (
        queries.astype(jnp.float32) + jnp.dot(attended, w_mix, preferred_element_type=jnp.float32)
    ).astype(jnp.bfloat16)
    mix_term = lax.dot_general(
        attended, cotangent, (((0,), (0,)), ((), ())), preferred_element_type=jnp.float32
    )
    out_grad = lax.psum(mix_term, ("section", "ray", "dp"))
    attn_grad = lax.dot_general(
        cotangent, w_mix, (((1,), (1,)), ((), ())), preferred_element_type=jnp.float32
    )
    attn_grad = attn_grad.astype(jnp.bfloat16).reshape(ray_rows, HEADS, head_dim)
    prob_grad = jnp.einsum("rhd,lhd->hrl", attn_grad, values, preferred_element_type=jnp.float32)
    delta = jnp.sum(probs * prob_grad, -1, keepdims=True)
    score_grad = (probs * (prob_grad - delta) * scale).astype(jnp.bfloat16)
    count = latent.shape[0] * lax.axis_size("ray")
    key_grad = jnp.einsum(
        "hrl,rhd->lhd", score_grad, query, preferred_element_type=jnp.float32
    ).reshape(count, width)
    value_grad = jnp.einsum(
        "hrl,rhd->lhd", probs_low, attn_grad, preferred_element_type=jnp.float32
    ).reshape(count, width)
    stacked = jnp.stack([key_grad, value_grad], 1)
    pair_rows = lax.psum_scatter(
        stacked.astype(jnp.bfloat16), "ray", scatter_dimension=0, tiled=True
    )
    pair_sum = lax.psum(pair_rows, "section")
    latent_grad = latent_rows(pair_sum, w_pairs)
    return (handed[None, None], finished[None], features[None], latent_grad[None], out_grad)


def solution(mesh):
    return jax.shard_map(
        local,
        mesh=mesh,
        in_specs=(
            P("section", "dp", "ray", None),
            P("section", None),
            P("section", None, None, "ray"),
            P("section", "ray", None),
            P("section", None),
            P("section", None, "ray"),
            P("section", "ray", None),
            P("dp", "ray", None),
            P("dp", ("section", "ray"), None),
            P("section", None),
            P("section", None, None),
            P("section", None),
            P("dp", ("section", "ray"), None),
        ),
        out_specs=(
            P("section", "dp", "ray", None),
            P("dp", "ray", "section"),
            P("dp", ("section", "ray"), None),
            P("dp", "ray", None),
            P(),
        ),
        check_vma=False,
    )
```

profile of v0, /device:TPU:2, one launch (start us, length us, event | category | flops | bytes accessed | tf_op | source)
XLA Modules:
  0.0 928.3 jit_solution(4946242236666145838)
XLA Ops:
  8.1 1.1 convert_reduce_fusion.1
  9.2 1.2 fusion.73
  10.4 1.9 fusion.75
  12.3 0.0 reduce-scatter.6.cloned.1.call-start
  12.4 1.4 copy.44
  13.8 42.5 %all-gather.7.cloned.1.call-done = bf16[1024,1024]{1,0:T(8,128)(2,1)} async-done(((bf16[128,1024]{1,0:T(8,128)(2,1)}), bf16[1024,1024]{1,0:T(8,128)(2,1)}) %all-gather.7.cloned.1.call-update) | async-done | bytes 2097168 | tf_op jit(solution)/shard_map/all_gather | solution.py:89
  56.3 2.6 convolution_convert_fusion.3
  58.9 4.9 fusion.97
  63.7 4.3 fusion.48
  68.1 2.1 convolution_convert_fusion.2
  70.1 0.0 all-gather.11.cloned.1.call-start
  70.2 0.5 all-gather.11.cloned.1.call-update
  70.7 0.0 all-gather.15.cloned.1.call-start
  70.8 0.5 all-gather.15.cloned.1.call-update
  71.3 0.0 all-gather.17.cloned.1.call-start
  71.4 0.5 all-gather.17.cloned.1.call-update
  71.9 0.0 all-gather.9.cloned.1.call-start
  71.9 39.7 %reduce-scatter.6.cloned.1.call-done = bf16[128,1024]{1,0:T(8,128)(2,1)} async-done(((bf16[1024,1024]{1,0:T(8,128)(2,1)}), bf16[128,1024]{1,0:T(8,128)(2,1)}) %reduce-scatter.6.cloned.1.call-update) | async-done | bytes 262160 | tf_op jit(solution)/shard_map/reduce_scatter | solution.py:92
  111.7 1.1 convert_reduce_fusion
  112.8 0.2 fusion.70
  113.0 0.9 fusion.72
  114.0 0.0 all-gather.13.cloned.1.call-start
  114.0 18.6 %all-gather.11.cloned.1.call-done = bf16[1024,2,1024]{2,1,0:T(2,128)(2,1)} async-done(((bf16[64,2,1024]{2,1,0:T(2,128)(2,1)}), bf16[1024,2,1024]{2,1,0:T(2,128)(2,1)}) %all-gather.11.cloned.1.call-update) | async-done | bytes 4194320 | tf_op jit(solution)/shard_map/all_gather | solution.py:124
  132.7 11.1 %copy.47 = bf16[1024,2,1024]{0,2,1:T(8,128)(2,1)} copy(bf16[1024,2,1024]{2,1,0:T(2,128)(2,1)} %all-gather.11.cloned.1.call-done) | data formatting | bytes 8388608 | tf_op jit(solution)/shard_map/all_gather | solution.py:124
  143.8 4.6 convolution_convert_fusion
  148.5 0.0 reduce-scatter.8.cloned.1.call-start
  148.5 39.0 %all-gather.15.cloned.1.call-done = bf16[1024,1024]{1,0:T(8,128)(2,1)} async-done(((bf16[64,1024]{1,0:T(8,128)(2,1)}), bf16[1024,1024]{1,0:T(8,128)(2,1)}) %all-gather.15.cloned.1.call-update) | async-done | bytes 2097168 | tf_op jit(solution)/shard_map/all_gather | solution.py:123
  187.5 2.3 convolution_convert_fusion.5
  189.8 1.0 copy.49
  190.8 51.5 %all-gather.17.cloned.1.call-done = bf16[1024,1024]{1,0:T(8,128)(2,1)} async-done(((bf16[64,1024]{1,0:T(8,128)(2,1)}), bf16[1024,1024]{1,0:T(8,128)(2,1)}) %all-gather.17.cloned.1.call-update) | async-done | bytes 2097168 | tf_op jit(solution)/shard_map/all_gather | solution.py:125
  242.3 2.3 convolution_convert_fusion.4
  244.6 1.0 copy.51
  245.6 39.2 %all-gather.9.cloned.1.call-done = bf16[1024,1024]{1,0:T(8,128)(2,1)} async-done(((bf16[128,1024]{1,0:T(8,128)(2,1)}), bf16[1024,1024]{1,0:T(8,128)(2,1)}) %all-gather.9.cloned.1.call-update) | async-done | bytes 2097168 | tf_op jit(solution)/shard_map/all_gather | solution.py:101
  284.9 5.8 convolution_convert_fusion.1
  290.7 0.2 reduce-scatter.10.cloned.1.call-start
  290.9 66.2 %all-gather.13.cloned.1.call-done = bf16[1024,2048]{1,0:T(8,128)(2,1)} async-done(((bf16[128,2048]{1,0:T(8,128)(2,1)}), bf16[1024,2048]{1,0:T(8,128)(2,1)}) %all-gather.13.cloned.1.call-update) | async-done | bytes 4194320 | tf_op jit(solution)/shard_map/all_gather | solution.py:131
  357.2 4.0 fusion.96
  361.2 2.6 copy.50
  363.8 2.9 copy.48
  366.7 9.8 %fusion.98 = (f32[16,256]{1,0:T(8,128)S(1)}, f32[16,256,1024]{2,1,0:T(8,128)}) fusion(bf16[256,16,64]{0,2,1:T(8,128)(2,1)S(1)} %bitcast.149, bf16[1024,16,64]{0,2,1:T(8,128)(2,1)} %bitcast.144), kind=kOutput, calls=%fused_computation.110 | convolution fusion | flops 549454848 | bytes 19415040 | tf_op jit(solution)/shard_map/sub | solution.py:30
  376.5 8.1 fusion.99
  384.5 38.2 %fusion.38 = bf16[16,64,1024]{2,1,0:T(8,128)(2,1)} fusion(bf16[256,16,64]{0,2,1:T(8,128)(2,1)S(1)} %bitcast.150, f32[16,256,1024]{2,1,0:T(8,128)} %fusion.99, f32[16,256,1024]{2,1,0:T(8,128)} %get-tuple-element.18, f32[16,256]{1,0:T(8,128)S(1)} %get-tuple-element.17), kind=kOutput, calls=%fused_computation.40 | convolution fusion | flops 567284736 | bytes 36192256 | tf_op jit(solution)/shard_map/hrl,rhd->lhd/dot_general | solution.py:170
  422.8 7.1 fusion.35
  429.9 2.4 pad_maximum_fusion
  432.3 6.5 copy.57
  438.8 0.0 all-reduce.6.cloned.1.call-start
  438.9 1.9 broadcast_select_fusion
  440.8 52.2 %reduce-scatter.10.cloned.1.call-done = bf16[128,2048]{1,0:T(8,128)(2,1)} async-done(((bf16[1024,2048]{1,0:T(8,128)(2,1)}), bf16[128,2048]{1,0:T(8,128)(2,1)}) %reduce-scatter.10.cloned.1.call-update) | async-done | bytes 524304
  492.9 2.0 copy.58
  495.0 0.3 all-reduce.4.cloned.1.call-start
  495.3 8.5 fusion.42
  503.8 2.7 fusion.78
  506.5 10.0 %fusion.95 = (bf16[1024,1,1024]{2,1,0:T(2,128)(2,1)}, bf16[1024,1,1024]{2,1,0:T(2,128)(2,1)}) fusion(bf16[1024,2,1024]{2,1,0:T(2,128)(2,1)} %all-gather.11.cloned.1.call-done), kind=kLoop, calls=%fused_computation.107 | loop fusion | bytes 8388608 | tf_op jit(solution)/shard_map/slice | solution.py:49
  516.5 1.9 collective-permute-start
  518.5 1.5 fusion.45
  520.0 4.7 collective-permute-done
  524.7 109.9 %all-reduce.6.cloned.1.call-done = (bf16[128,1024]{1,0:T(8,128)(2,1)}, bf16[128,2,1024]{0,2,1:T(8,128)(2,1)}) async-done(((bf16[128,1024]{1,0:T(8,128)(2,1)}, bf16[128,2,1024]{0,2,1:T(8,128)(2,1)}), (bf16[128,1024]{1,0:T(8,128)(2,1)}, bf16[128,2,1024]{0,2,1:T(8,128)(2,1)})) %all-reduce.6.cloned.1.call-update) | async-done | bytes 786448 | tf_op jit(solution)/shard_map/psum | solution.py:18
  634.6 0.8 constant_dynamic-slice_fusion
  635.5 0.7 copy.46
  636.2 3.1 fusion.33
  639.3 3.9 fusion.49
  643.2 272.5 %all-reduce.4.cloned.1.call-done = f32[1024,1024]{1,0:T(8,128)} async-done(((f32[1024,1024]{1,0:T(8,128)}), f32[1024,1024]{1,0:T(8,128)}) %all-reduce.4.cloned.1.call-update) | async-done | bytes 4194320 | tf_op jit(solution)/shard_map/psum | solution.py:161
  915.7 0.7 copy.75
  916.4 4.8 copy.76
  (44 shorter events, 0.3 us)
Async XLA Ops:
  8.0 276.9 %copy-start = (bf16[1,512,1024]{2,1,0:T(8,128)(2,1)S(1)}, bf16[1,512,1024]{2,1,0:T(8,128)(2,1)}, u32[]{:S(2)}) copy-start(bf16[1,512,1024]{2,1,0:T(8,128)(2,1)} %param.19) | copy-start | bytes 3145732
  8.0 48.2 %all-gather.7.cloned.1.call-start = ((), (), s32[]{:S(2)}) async-start(), calls=%async_computation.3 | async-start | bytes 2359296 | tf_op jit(solution)/shard_map/all_gather | solution.py:89
  12.3 99.4 %reduce-scatter.6.cloned.1.call-start = ((), (), s32[]{:S(2)}) async-start(), calls=%async_computation.4 | async-start | bytes 2359296 | tf_op jit(solution)/shard_map/reduce_scatter | solution.py:92
  63.7 4.3 copy-start.11
  68.0 43.6 %copy-start.2 = (bf16[1,1,128,1024]{3,2,1,0:T(8,128)(2,1)S(1)}, bf16[1,1,128,1024]{3,2,1,0:T(8,128)(2,1)}, u32[]{:S(2)}) copy-start(bf16[1,1,128,1024]{3,2,1,0:T(8,128)(2,1)} %param.13) | copy-start | bytes 786436
  68.0 45.0 %copy-start.14 = (f32[1,1024]{1,0:T(1,128)S(1)}, f32[1,1024]{1,0:T(1,128)}, u32[]{:S(2)}) copy-start(f32[1,1024]{1,0:T(1,128)} %param.17) | copy-start | bytes 12292
  70.1 62.5 %all-gather.11.cloned.1.call-start = ((), (), s32[]{:S(2)}) async-start(), calls=%async_computation.7 | async-start | bytes 4456448 | tf_op jit(solution)/shard_map/all_gather | solution.py:124
  70.7 116.8 %all-gather.15.cloned.1.call-start = ((), (), s32[]{:S(2)}) async-start(), calls=%async_computation.9 | async-start | bytes 2228224 | tf_op jit(solution)/shard_map/all_gather | solution.py:123
  71.3 171.0 %all-gather.17.cloned.1.call-start = ((), (), s32[]{:S(2)}) async-start(), calls=%async_computation.10 | async-start | bytes 2228224 | tf_op jit(solution)/shard_map/all_gather | solution.py:125
  71.9 213.0 %all-gather.9.cloned.1.call-start = ((), (), s32[]{:S(2)}) async-start(), calls=%async_computation.5 | async-start | bytes 2359296 | tf_op jit(solution)/shard_map/all_gather | solution.py:101
  114.0 29.8 %copy-start.12 = (bf16[1,128,1024]{2,1,0:T(8,128)(2,1)S(1)}, bf16[1,128,1024]{2,1,0:T(8,128)(2,1)}, u32[]{:S(2)}) copy-start(bf16[1,128,1024]{2,1,0:T(8,128)(2,1)} %param.20) | copy-start | bytes 786436
  114.0 243.2 %all-gather.13.cloned.1.call-start = ((), (), s32[]{:S(2)}) async-start(), calls=%async_computation.8 | async-start | bytes 4718592 | tf_op jit(solution)/shard_map/all_gather | solution.py:131
  143.8 43.7 %copy-start.8 = (bf16[1,256,1024]{2,1,0:T(8,128)(2,1)S(1)}, bf16[1,256,1024]{2,1,0:T(8,128)(2,1)}, u32[]{:S(2)}) copy-start(bf16[1,256,1024]{2,1,0:T(8,128)(2,1)} %param.21) | copy-start | bytes 1572868
  143.8 98.5 %copy-start.6 = (bf16[1,256,1024]{2,1,0:T(8,128)(2,1)S(1)}, bf16[1,256,1024]{2,1,0:T(8,128)(2,1)}, u32[]{:S(2)}) copy-start(bf16[1,256,1024]{2,1,0:T(8,128)(2,1)} %param.25) | copy-start | bytes 1572868
  148.5 290.5 %reduce-scatter.8.cloned.1.call-start = ((), (), s32[]{:S(2)}) async-start(), calls=%async_computation.6 | async-start | bytes 2359296 | tf_op jit(solution)/shard_map/reduce_scatter | solution.py:109
  290.7 202.2 %reduce-scatter.10.cloned.1.call-start = ((), (), s32[]{:S(2)}) async-start(), calls=%async_computation.12 | async-start | bytes 4718592
  361.2 5.4 copy-start.10
  366.6 9.8 %copy-start.4 = (bf16[256,1024]{0,1:T(8,128)(2,1)S(1)}, bf16[256,1024]{0,1:T(8,128)(2,1)}, u32[]{:S(2)}) copy-start(bf16[256,1024]{0,1:T(8,128)(2,1)} %copy.51) | copy-start | bytes 1572868
  422.8 7.1 copy-start.5
  438.8 195.8 %all-reduce.6.cloned.1.call-start = ((), (), s32[]{:S(2)}) async-start(), calls=%async_computation.13 | async-start | bytes 1572864 | tf_op jit(solution)/shard_map/psum | solution.py:18
  495.0 8.8 copy-start.7
  495.0 420.7 %all-reduce.4.cloned.1.call-start = ((), (), s32[]{:S(2)}) async-start(), calls=%async_computation.11 | async-start | bytes 8388608 | tf_op jit(solution)/shard_map/psum | solution.py:161
  506.5 10.0 %copy-start.13 = (bf16[128,1024]{1,0:T(8,128)(2,1)S(1)}, bf16[128,1024]{1,0:T(8,128)(2,1)}, u32[]{:S(2)}) copy-start(bf16[128,1024]{1,0:T(8,128)(2,1)} %get-tuple-element.8) | copy-start | bytes 786436
  506.5 11.9 %copy-start.3 = (bf16[1024,1024]{1,0:T(8,128)(2,1)S(1)}, bf16[1024,1024]{1,0:T(8,128)(2,1)}, u32[]{:S(2)}) copy-start(bf16[1024,1024]{1,0:T(8,128)(2,1)} %all-gather.17.cloned.1.call-done) | copy-start | bytes 6291460
  506.5 11.9 %copy-start.9 = (bf16[1,256,1024]{2,1,0:T(8,128)(2,1)S(1)}, bf16[1,256,1024]{2,1,0:T(8,128)(2,1)}, u32[]{:S(2)}) copy-start(bf16[1,256,1024]{2,1,0:T(8,128)(2,1)} %param.21) | copy-start | bytes 1572868
  516.5 8.2 collective-permute-start
  915.7 5.5 copy-start.1
Sparse Core Ops, SparseCore 0:
  12.4 43.7 all-gather.6
  70.3 41.3 reduce-scatter.5
  290.8 69.1 reduce-scatter.7
  439.0 53.9 reduce-scatter.9
Sparse Core Ops, SparseCore 1:
  73.4 59.3 all-gather.10
  135.3 52.1 all-gather.14
  190.1 52.1 all-gather.16
  244.7 40.1 all-gather.8
  286.7 70.4 all-gather.12
  495.1 139.5 all-reduce.5
  640.0 275.7 all-reduce.3
where the time goes:
time: 929 us; the launch traced here: 928 us
  waiting for transfers between devices  738 us (79%)
  matrix products  112 us (12%)
  local copies, waits for them, and re-layouts  49.6 us (5%)
  between operations  15.6 us (2%)
  other arithmetic  10.7 us (1%)
    psum x1, waiting for transfers between devices, local(): out_grad = lax.psum(mix_term, ('section', 'ray', 'dp'))  273 us
    psum x1, waiting for transfers between devices, spread_2(): return lax.psum(jnp.where(mine, value, jnp.zeros_like(value)), axis)  110 us
    all_gather x1, waiting for transfers between devices, local(): lax.all_gather(jnp.dot(latent, flat_pairs, preferred_element_type=jnp.flo...  66.2 us
    unnamed x12, waiting for transfers between devices  53.9 us
    all_gather x1, waiting for transfers between devices, local(): lax.all_gather(dec_out, 'section', axis=0, tiled=True)  51.5 us
    all_gather x1, waiting for transfers between devices, local(): lax.all_gather(normed, 'ray', axis=0, tiled=True)  42.5 us
    reduce_scatter x1, waiting for transfers between devices, local(): lax.psum_scatter(jnp.dot(mixed, w_attn_out, preferred_element_type=jnp.fl...  39.7 us
    all_gather x1, waiting for transfers between devices, local(): lax.all_gather(layer_norm(hidden, gain_two).astype(jnp.bfloat16), 'ray',...  39.2 us
  transfers between devices with their start and end apart: 12, of which 11 were waited for; matrix products, arithmetic and copies ran while one was open for 16% of the time, Pallas kernels for 0%

commit v1 on v0

--- a/solution.py
+++ b/solution.py
@@ -5,6 +5,11 @@
 from jax.sharding import PartitionSpec as P
 
 HEADS = 16
+
+
+def swapped_in(x, mesh_axis, d):
+    sent = jnp.stack([x] * lax.axis_size(mesh_axis))
+    return jnp.concatenate(lax.all_to_all(sent, mesh_axis, 0, 0), axis=d)
 
 
 def shifted(value, axis, by):
@@ -122,7 +127,7 @@
     w_query, w_pairs, w_mix = (
         lax.all_gather(dec_query, "section", axis=0, tiled=True),
         lax.all_gather(dec_kv, "section", axis=0, tiled=True),
-        lax.all_gather(dec_out, "section", axis=0, tiled=True),
+        swapped_in(dec_out, "section", 0),
     )
     latent = set_latent[0]
     queries = ray_queries[0]

time: 929 us -> 881 us (0.948)
  waiting for transfers between devices: 738 us -> 658 us
  blocking collectives: 0 us -> 31.8 us
    all_gather x1 -> x0, waiting for transfers between devices: 51.5 us -> none  [local(): lax.all_gather(dec_out, 'section', axis=0, tiled=True)]
    all_to_all x0 -> x1, blocking collectives: none -> 31.8 us  [swapped_in(): return jnp.concatenate(lax.all_to_all(sent, mesh_axis, 0, 0), axis=d)]
    all_gather x1, waiting for transfers between devices: 39 us -> 10.6 us  [local(): lax.all_gather(dec_query, 'section', axis=0, tiled=True)]
    unnamed x12 -> x11, waiting for transfers between devices: 53.9 us -> 53.3 us
  transfers between devices with their start and end apart: 12 -> 11, of which waited for: 11 -> 10; matrix products, arithmetic and copies ran while one was open for 16% -> 16% of each run, Pallas kernels for 0% -> 0%
where the time goes in v1:
time: 881 us; the launch traced here: 880 us
  waiting for transfers between devices  658 us (75%)
  matrix products  110 us (12%)
  local copies, waits for them, and re-layouts  51.2 us (6%)
  blocking collectives  31.8 us (4%)
  between operations  15.6 us (2%)
  other arithmetic  10.7 us (1%)
    psum x1, waiting for transfers between devices, local(): out_grad = lax.psum(mix_term, ('section', 'ray', 'dp'))  273 us
    psum x1, waiting for transfers between devices, spread_2(): return lax.psum(jnp.where(mine, value, jnp.zeros_like(value)), axis)  110 us
    all_gather x1, waiting for transfers between devices, local(): lax.all_gather(jnp.dot(latent, flat_pairs, preferred_element_type=jnp.flo...  66.2 us
    unnamed x11, waiting for transfers between devices  53.3 us
    all_gather x1, waiting for transfers between devices, local(): lax.all_gather(normed, 'ray', axis=0, tiled=True)  42.5 us
    reduce_scatter x1, waiting for transfers between devices, local(): lax.psum_scatter(jnp.dot(mixed, w_attn_out, preferred_element_type=jnp.fl...  40.3 us
    all_gather x1, waiting for transfers between devices, local(): lax.all_gather(layer_norm(hidden, gain_two).astype(jnp.bfloat16), 'ray',...  39.4 us
    dot_general x1, matrix products, local(): jnp.einsum('hrl,rhd->lhd', score_grad, query, preferred_element_type=jnp....  38.2 us
  transfers between devices with their start and end apart: 11, of which 10 were waited for; matrix products, arithmetic and copies ran while one was open for 16% of the time, Pallas kernels for 0%

profile of v1, /device:TPU:2, one launch (start us, length us, event | category | flops | bytes accessed | tf_op | source)
XLA Modules:
  0.0 880.2 jit_solution(10256089633738596450)
XLA Ops:
  8.1 1.1 convert_reduce_fusion.1
  9.2 1.2 fusion.74
  10.4 1.9 fusion.76
  12.3 0.0 reduce-scatter.6.cloned.1.call-start
  12.4 1.4 copy.44
  13.8 42.5 %all-gather.6.cloned.1.call-done = bf16[1024,1024]{1,0:T(8,128)(2,1)} async-done(((bf16[128,1024]{1,0:T(8,128)(2,1)}), bf16[1024,1024]{1,0:T(8,128)(2,1)}) %all-gather.6.cloned.1.call-update) | async-done | bytes 2097168 | tf_op jit(solution)/shard_map/all_gather | solution.py:94
  56.3 2.6 convolution_convert_fusion.3
  58.9 4.9 fusion.99
  63.8 4.3 fusion.49
  68.1 2.1 convolution_convert_fusion.2
  70.1 0.0 all-gather.10.cloned.1.call-start
  70.2 0.5 all-gather.10.cloned.1.call-update
  70.7 0.0 all-gather.14.cloned.1.call-start
  70.8 0.5 all-gather.14.cloned.1.call-update
  71.3 0.0 all-gather.8.cloned.1.call-start
  71.4 40.3 %reduce-scatter.6.cloned.1.call-done = bf16[128,1024]{1,0:T(8,128)(2,1)} async-done(((bf16[1024,1024]{1,0:T(8,128)(2,1)}), bf16[128,1024]{1,0:T(8,128)(2,1)}) %reduce-scatter.6.cloned.1.call-update) | async-done | bytes 262160 | tf_op jit(solution)/shard_map/reduce_scatter | solution.py:97
  111.7 1.1 convert_reduce_fusion
  112.8 0.2 fusion.71
  113.1 0.9 fusion.73
  114.0 0.0 all-gather.12.cloned.1.call-start
  114.1 18.6 %all-gather.10.cloned.1.call-done = bf16[1024,2,1024]{2,1,0:T(2,128)(2,1)} async-done(((bf16[64,2,1024]{2,1,0:T(2,128)(2,1)}), bf16[1024,2,1024]{2,1,0:T(2,128)(2,1)}) %all-gather.10.cloned.1.call-update) | async-done | bytes 4194320 | tf_op jit(solution)/shard_map/all_gather | solution.py:129
  132.7 11.1 %copy.47 = bf16[1024,2,1024]{0,2,1:T(8,128)(2,1)} copy(bf16[1024,2,1024]{2,1,0:T(2,128)(2,1)} %all-gather.10.cloned.1.call-done) | data formatting | bytes 8388608 | tf_op jit(solution)/shard_map/all_gather | solution.py:129
  143.8 4.6 convolution_convert_fusion
  148.4 0.0 reduce-scatter.8.cloned.1.call-start
  148.5 0.3 stack.5
  148.7 31.8 %all_to_all.5 = bf16[16,64,1024]{2,1,0:T(8,128)(2,1)S(1)} all-to-all(bf16[16,64,1024]{2,1,0:T(8,128)(2,1)S(1)} %stack.5), channel_id=1, replica_groups=mesh['section'=16,'ray'=8,'dp'=2] {'section'}, dimensions={0} | all-to-all | bytes 4194304 | tf_op jit(solution)/shard_map/all_to_all | solution.py:12
  180.5 1.3 copy-done.2
  181.8 0.8 convolution_convert_fusion.4
  182.6 1.0 copy.51
  183.6 10.6 %all-gather.14.cloned.1.call-done = bf16[1024,1024]{1,0:T(8,128)(2,1)} async-done(((bf16[64,1024]{1,0:T(8,128)(2,1)}), bf16[1024,1024]{1,0:T(8,128)(2,1)}) %all-gather.14.cloned.1.call-update) | async-done | bytes 2097168 | tf_op jit(solution)/shard_map/all_gather | solution.py:128
  194.2 2.3 convolution_convert_fusion.5
  196.5 1.0 copy.49
  197.5 39.4 %all-gather.8.cloned.1.call-done = bf16[1024,1024]{1,0:T(8,128)(2,1)} async-done(((bf16[128,1024]{1,0:T(8,128)(2,1)}), bf16[1024,1024]{1,0:T(8,128)(2,1)}) %all-gather.8.cloned.1.call-update) | async-done | bytes 2097168 | tf_op jit(solution)/shard_map/all_gather | solution.py:106
  236.9 5.8 convolution_convert_fusion.1
  242.7 0.2 reduce-scatter.10.cloned.1.call-start
  242.9 66.2 %all-gather.12.cloned.1.call-done = bf16[1024,2048]{1,0:T(8,128)(2,1)} async-done(((bf16[128,2048]{1,0:T(8,128)(2,1)}), bf16[1024,2048]{1,0:T(8,128)(2,1)}) %all-gather.12.cloned.1.call-update) | async-done | bytes 4194320 | tf_op jit(solution)/shard_map/all_gather | solution.py:136
  309.2 4.0 fusion.98
  313.2 2.6 copy.50
  315.8 2.9 copy.48
  318.6 9.8 %fusion.100 = (f32[16,256]{1,0:T(8,128)S(1)}, f32[16,256,1024]{2,1,0:T(8,128)}) fusion(bf16[256,16,64]{0,2,1:T(8,128)(2,1)S(1)} %bitcast.159, bf16[1024,16,64]{0,2,1:T(8,128)(2,1)} %bitcast.154), kind=kOutput, calls=%fused_computation.112 | convolution fusion | flops 549454848 | bytes 19415040 | tf_op jit(solution)/shard_map/sub | solution.py:35
  328.5 8.1 fusion.101
  336.6 38.2 %fusion.38 = bf16[16,64,1024]{2,1,0:T(8,128)(2,1)} fusion(bf16[256,16,64]{0,2,1:T(8,128)(2,1)S(1)} %bitcast.160, f32[16,256,1024]{2,1,0:T(8,128)} %fusion.101, f32[16,256,1024]{2,1,0:T(8,128)} %get-tuple-element.18, f32[16,256]{1,0:T(8,128)S(1)} %get-tuple-element.17), kind=kOutput, calls=%fused_computation.40 | convolution fusion | flops 567284736 | bytes 36192256 | tf_op jit(solution)/shard_map/hrl,rhd->lhd/dot_general | solution.py:175
  374.7 7.1 fusion.35
  381.9 2.4 pad_maximum_fusion
  384.2 6.5 copy.57
  390.8 0.0 all-reduce.6.cloned.1.call-start
  390.9 1.9 broadcast_select_fusion
  392.7 52.1 %reduce-scatter.10.cloned.1.call-done = bf16[128,2048]{1,0:T(8,128)(2,1)} async-done(((bf16[1024,2048]{1,0:T(8,128)(2,1)}), bf16[128,2048]{1,0:T(8,128)(2,1)}) %reduce-scatter.10.cloned.1.call-update) | async-done | bytes 524304
  444.9 2.1 copy.58
  447.0 0.3 all-reduce.4.cloned.1.call-start
  447.2 8.5 fusion.43
  455.7 2.7 fusion.79
  458.5 10.0 %fusion.97 = (bf16[1024,1,1024]{2,1,0:T(2,128)(2,1)}, bf16[1024,1,1024]{2,1,0:T(2,128)(2,1)}) fusion(bf16[1024,2,1024]{2,1,0:T(2,128)(2,1)} %all-gather.10.cloned.1.call-done), kind=kLoop, calls=%fused_computation.109 | loop fusion | bytes 8388608 | tf_op jit(solution)/shard_map/slice | solution.py:54
  468.5 1.9 collective-permute-start
  470.4 1.5 fusion.46
  472.0 4.7 collective-permute-done
  476.7 109.7 %all-reduce.6.cloned.1.call-done = (bf16[128,1024]{1,0:T(8,128)(2,1)}, bf16[128,2,1024]{0,2,1:T(8,128)(2,1)}) async-done(((bf16[128,1024]{1,0:T(8,128)(2,1)}, bf16[128,2,1024]{0,2,1:T(8,128)(2,1)}), (bf16[128,1024]{1,0:T(8,128)(2,1)}, bf16[128,2,1024]{0,2,1:T(8,128)(2,1)})) %all-reduce.6.cloned.1.call-update) | async-done | bytes 786448 | tf_op jit(solution)/shard_map/psum | solution.py:23
  586.4 0.8 constant_dynamic-slice_fusion
  587.2 0.7 copy.46
  587.9 3.1 fusion.33
  591.1 3.9 fusion.50
  594.9 272.7 %all-reduce.4.cloned.1.call-done = f32[1024,1024]{1,0:T(8,128)} async-done(((f32[1024,1024]{1,0:T(8,128)}), f32[1024,1024]{1,0:T(8,128)}) %all-reduce.4.cloned.1.call-update) | async-done | bytes 4194320 | tf_op jit(solution)/shard_map/psum | solution.py:166
  867.6 0.7 copy.75
  868.3 4.8 copy.76
  (47 shorter events, 0.3 us)
Async XLA Ops:
  8.0 228.9 %copy-start = (bf16[1,512,1024]{2,1,0:T(8,128)(2,1)S(1)}, bf16[1,512,1024]{2,1,0:T(8,128)(2,1)}, u32[]{:S(2)}) copy-start(bf16[1,512,1024]{2,1,0:T(8,128)(2,1)} %param.19) | copy-start | bytes 3145732
  8.0 48.2 %all-gather.6.cloned.1.call-start = ((), (), s32[]{:S(2)}) async-start(), calls=%async_computation.4 | async-start | bytes 2359296 | tf_op jit(solution)/shard_map/all_gather | solution.py:94
  12.3 99.4 %reduce-scatter.6.cloned.1.call-start = ((), (), s32[]{:S(2)}) async-start(), calls=%async_computation.5 | async-start | bytes 2359296 | tf_op jit(solution)/shard_map/reduce_scatter | solution.py:97
  63.7 4.3 copy-start.12
  68.0 43.7 %copy-start.4 = (bf16[1,1,128,1024]{3,2,1,0:T(8,128)(2,1)S(1)}, bf16[1,1,128,1024]{3,2,1,0:T(8,128)(2,1)}, u32[]{:S(2)}) copy-start(bf16[1,1,128,1024]{3,2,1,0:T(8,128)(2,1)} %param.13) | copy-start | bytes 786436
  68.0 45.0 %copy-start.16 = (f32[1,1024]{1,0:T(1,128)S(1)}, f32[1,1024]{1,0:T(1,128)}, u32[]{:S(2)}) copy-start(f32[1,1024]{1,0:T(1,128)} %param.17) | copy-start | bytes 12292
  70.1 62.5 %all-gather.10.cloned.1.call-start = ((), (), s32[]{:S(2)}) async-start(), calls=%async_computation.8 | async-start | bytes 4456448 | tf_op jit(solution)/shard_map/all_gather | solution.py:129
  70.7 123.4 %all-gather.14.cloned.1.call-start = ((), (), s32[]{:S(2)}) async-start(), calls=%async_computation.10 | async-start | bytes 2228224 | tf_op jit(solution)/shard_map/all_gather | solution.py:128
  71.3 165.6 %all-gather.8.cloned.1.call-start = ((), (), s32[]{:S(2)}) async-start(), calls=%async_computation.6 | async-start | bytes 2359296 | tf_op jit(solution)/shard_map/all_gather | solution.py:106
  114.0 29.8 %copy-start.13 = (bf16[1,128,1024]{2,1,0:T(8,128)(2,1)S(1)}, bf16[1,128,1024]{2,1,0:T(8,128)(2,1)}, u32[]{:S(2)}) copy-start(bf16[1,128,1024]{2,1,0:T(8,128)(2,1)} %param.20) | copy-start | bytes 786436
  114.0 195.2 %all-gather.12.cloned.1.call-start = ((), (), s32[]{:S(2)}) async-start(), calls=%async_computation.9 | async-start | bytes 4718592 | tf_op jit(solution)/shard_map/all_gather | solution.py:136
  143.8 4.6 copy-start.15
  148.4 33.4 %copy-start.7 = (bf16[1,256,1024]{2,1,0:T(8,128)(2,1)S(1)}, bf16[1,256,1024]{2,1,0:T(8,128)(2,1)}, u32[]{:S(2)}) copy-start(bf16[1,256,1024]{2,1,0:T(8,128)(2,1)} %param.25) | copy-start | bytes 1572868
  148.4 242.5 %reduce-scatter.8.cloned.1.call-start = ((), (), s32[]{:S(2)}) async-start(), calls=%async_computation.7 | async-start | bytes 2359296 | tf_op jit(solution)/shard_map/reduce_scatter | solution.py:114
  148.7 45.4 %copy-start.9 = (bf16[1,256,1024]{2,1,0:T(8,128)(2,1)S(1)}, bf16[1,256,1024]{2,1,0:T(8,128)(2,1)}, u32[]{:S(2)}) copy-start(bf16[1,256,1024]{2,1,0:T(8,128)(2,1)} %param.21) | copy-start | bytes 1572868
  180.5 1.3 copy-start.2
  242.7 202.2 %reduce-scatter.10.cloned.1.call-start = ((), (), s32[]{:S(2)}) async-start(), calls=%async_computation.12 | async-start | bytes 4718592
  313.2 5.4 copy-start.11
  318.6 9.8 %copy-start.5 = (bf16[256,1024]{0,1:T(8,128)(2,1)S(1)}, bf16[256,1024]{0,1:T(8,128)(2,1)}, u32[]{:S(2)}) copy-start(bf16[256,1024]{0,1:T(8,128)(2,1)} %copy.51) | copy-start | bytes 1572868
  374.7 7.1 copy-start.6
  390.8 195.6 %all-reduce.6.cloned.1.call-start = ((), (), s32[]{:S(2)}) async-start(), calls=%async_computation.13 | async-start | bytes 1572864 | tf_op jit(solution)/shard_map/psum | solution.py:23
  446.9 8.8 copy-start.8
  447.0 420.6 %all-reduce.4.cloned.1.call-start = ((), (), s32[]{:S(2)}) async-start(), calls=%async_computation.11 | async-start | bytes 8388608 | tf_op jit(solution)/shard_map/psum | solution.py:166
  458.4 10.0 %copy-start.14 = (bf16[128,1024]{1,0:T(8,128)(2,1)S(1)}, bf16[128,1024]{1,0:T(8,128)(2,1)}, u32[]{:S(2)}) copy-start(bf16[128,1024]{1,0:T(8,128)(2,1)} %get-tuple-element.8) | copy-start | bytes 786436
  458.5 11.9 %copy-start.3 = (bf16[16,64,1024]{2,1,0:T(8,128)(2,1)S(1)}, bf16[16,64,1024]{2,1,0:T(8,128)(2,1)}, u32[]{:S(2)}) copy-start(bf16[16,64,1024]{2,1,0:T(8,128)(2,1)} %copy-done.2) | copy-start | bytes 6291460
  458.5 11.9 %copy-start.10 = (bf16[1,256,1024]{2,1,0:T(8,128)(2,1)S(1)}, bf16[1,256,1024]{2,1,0:T(8,128)(2,1)}, u32[]{:S(2)}) copy-start(bf16[1,256,1024]{2,1,0:T(8,128)(2,1)} %param.21) | copy-start | bytes 1572868
  468.5 8.2 collective-permute-start
  867.6 5.5 copy-start.1
Sparse Core Ops, SparseCore 0:
  12.4 43.7 all-gather.5
  70.3 41.3 reduce-scatter.5
  242.8 69.1 reduce-scatter.7
  390.9 53.8 reduce-scatter.9
Sparse Core Ops, SparseCore 1:
  73.4 59.3 all-gather.9
  135.3 58.8 all-gather.13
  196.4 40.4 all-gather.7
  238.7 70.4 all-gather.11
  447.0 139.3 all-reduce.5
  591.9 275.7 all-reduce.3
